TPU v7x, 32 devices: a whole 2x2x4 slice. The times are simulated.
32 devices in a mesh: groups: 2 (over x), gx: 16 (over z, y, core).
Axes of the slice: x: 2, y: 2, z: 4, core: 2. Of those that a mesh axis runs over, the one named last changes fastest.
Arguments:
- features: bfloat16 [64, 16, 64, 128], P(('groups', 'gx')), parts along dimension 0, may hold values from -6 to 6
- cotangent: bfloat16 [64, 16, 64, 128], P(('groups', 'gx')), parts along dimension 0, may hold values from -6 to 6
- wall_flags: int32 [64, 16, 128], P(('groups', 'gx')), parts along dimension 0, may hold values 0 or 1
- mode_counts: int32 [64], replicated, may hold values from 1 to 16, as said below
- offsets: int32 [6, 3], replicated, may hold values from -2 to 2, as said below
- point_weight: bfloat16 [64, 64], replicated, may hold values from -0.75 to 0.75
- kernel_weight: bfloat16 [6, 64, 64], replicated, may hold values from -0.3125 to 0.3125
- lap_weight: bfloat16 [64, 64], replicated, may hold values from -0.125 to 0.125
- spec_weight: bfloat16 [16, 64, 64], replicated, may hold values from -1 to 1
- bias: float32 [64], replicated, may hold values from -3 to 3
Outputs:
- input_grad: bfloat16 [64, 16, 64, 128], P(('groups', 'gx')), parts along dimension 0
- kernel_grad: float32 [12, 64, 64], P('groups'), parts along dimension 0
There are 2 independent parts, one for each index of `groups`. A program takes and returns all parts, laid end to end along the dimension named above; an argument that names none is the same for every part. Nothing has to cross between parts.
Inputs may be any that keep to these rules, and one draw needn't show every extreme that they name: Column 0 holds x offsets in -1..1 and both -1 and 1 occur; columns 1 and 2 hold y and z offsets in -2..2, and -2 and 2 occur in each of them. `mode_counts`: some channel keeps 16 modes and some channel keeps 1.
All inputs are finite; a program needn't handle non-finite values. No bound on the sum of `wall_flags` on one device may be relied on, other than what follows from the above.
Results may differ from a plain program's by a relative error of at most 0.0066.
Values may be sent and summed in bfloat16 or wider, within the bound.
A program may use at most 256 MiB of HBM per device.

v0:
```python
from functools import partial
import math
import jax
import jax.numpy as jnp
from jax import lax
from jax.sharding import PartitionSpec as P

RAD = 2


def with_halo(cells, sides, width):
    for axis, dim in sides:
        count = lax.axis_size(axis)
        ends = count - 1
        head = lax.slice_in_dim(cells, 0, width, axis=dim)
        tail = lax.slice_in_dim(cells, cells.shape[dim] - width, cells.shape[dim], axis=dim)
        cells = jnp.concatenate(
            [
                lax.ppermute(tail, axis, [(i, (i + 1) % count) for i in range(ends)]),
                cells,
                lax.ppermute(head, axis, [((i + 1) % count, i) for i in range(ends)]),
            ],
            axis=dim,
        )
    return cells


def basis_table(mode_total, length):
    mode_index = jnp.arange(mode_total, dtype=jnp.float32)[:, None]
    cell_index = jnp.arange(length, dtype=jnp.float32)[None, :]
    phase_angle = math.pi / (2.0 * length) * mode_index * (2.0 * cell_index + 1.0)
    amplitude = jnp.where(mode_index == 0.0, math.sqrt(1.0 / length), math.sqrt(2.0 / length))
    return (amplitude * jnp.cos(phase_angle)).astype(jnp.bfloat16)


def pencil_work(pencil, spec_weight, kept_modes, adjoint):
    basis = basis_table(spec_weight.shape[0], pencil.shape[0])
    coefficients = jnp.einsum(
        "kx,xycz->kycz", basis, pencil, preferred_element_type=jnp.float32
    ).astype(jnp.bfloat16)
    if adjoint:
        masked = coefficients * kept_modes[:, None, :, None].astype(jnp.bfloat16)
        mixed_modes = jnp.einsum(
            "koc,kyoz->kycz", spec_weight, masked, preferred_element_type=jnp.float32
        ).astype(jnp.bfloat16)
    else:
        mixed_modes = jnp.einsum(
            "koc,kycz->kyoz", spec_weight, coefficients, preferred_element_type=jnp.float32
        )
        mixed_modes = (mixed_modes * kept_modes[:, None, :, None]).astype(jnp.bfloat16)
    return jnp.einsum(
        "kx,kyoz->xyoz", basis, mixed_modes, preferred_element_type=jnp.float32
    ).astype(jnp.bfloat16)


def spectral(slab, spec_weight, kept_modes, adjoint):
    result = pencil_work(
        lax.all_to_all(slab, "gx", split_axis=1, concat_axis=0, tiled=True),
        spec_weight,
        kept_modes,
        adjoint,
    )
    return lax.all_to_all(result, "gx", split_axis=0, concat_axis=1, tiled=True)


def laplace_ext(extended):
    padded = jnp.pad(extended, ((0, 0), (1, 1), (0, 0), (1, 1))).astype(jnp.float32)
    centre_cells = padded[1:-1, 1:-1, :, 1:-1]
    neighbours = padded[2:, 1:-1, :, 1:-1] + padded[:-2, 1:-1, :, 1:-1]
    neighbours = neighbours + padded[1:-1, 2:, :, 1:-1] + padded[1:-1, :-2, :, 1:-1]
    neighbours = neighbours + padded[1:-1, 1:-1, :, 2:] + padded[1:-1, 1:-1, :, :-2]
    return (neighbours - 6.0 * centre_cells).astype(jnp.bfloat16)


def pad_sides(extended):
    return jnp.pad(extended, ((0, 0), (RAD, RAD), (0, 0), (RAD, RAD)))


def window_of(padded, offset, direction, slab_shape):
    starts = (
        1 + direction * offset[0],
        RAD + direction * offset[1],
        0,
        RAD + direction * offset[2],
    )
    return lax.dynamic_slice(padded, starts, slab_shape)


def gelu_slope(preact, upstream):
    _, pullback = jax.vjp(partial(jax.nn.gelu, approximate=True), preact)
    return pullback(upstream)[0]


def sum_over_gx(terms):
    count = lax.axis_size("gx")
    if terms.size % count:
        return lax.psum(terms, "gx")
    pieces = lax.all_to_all(terms.reshape(count, -1), "gx", split_axis=0, concat_axis=0, tiled=True)
    mine = jnp.sum(pieces, axis=0)
    copies = jnp.broadcast_to(mine[None, :], pieces.shape)
    gathered = lax.all_to_all(copies, "gx", split_axis=0, concat_axis=0, tiled=True)
    return gathered.reshape(terms.shape)


def per_device(
    features,
    cotangent,
    wall_flags,
    mode_counts,
    offsets,
    point_weight,
    kernel_weight,
    lap_weight,
    spec_weight,
    bias,
):
    mode_total = spec_weight.shape[0]
    tile_total = kernel_weight.shape[0]
    kept_modes = (jnp.arange(mode_total, dtype=jnp.int32)[:, None] < mode_counts[None, :]).astype(
        jnp.float32
    )
    fluid_mask = (1 - wall_flags).astype(jnp.float32)[:, :, None, :]
    extended = with_halo(features, (("gx", 0),), 1)
    padded_field = pad_sides(extended)
    local_part = jnp.einsum(
        "oc,xycz->xyoz", point_weight, features, preferred_element_type=jnp.float32
    )
    local_part = local_part + jnp.einsum(
        "oc,xycz->xyoz", lap_weight, laplace_ext(extended), preferred_element_type=jnp.float32
    )
    for tile in range(tile_total):
        moved = window_of(padded_field, offsets[tile], 1, features.shape)
        local_part = local_part + jnp.einsum(
            "oc,xycz->xyoz", kernel_weight[tile], moved, preferred_element_type=jnp.float32
        )
    local_part = local_part + bias[:, None]
    spectral_part = spectral(features, spec_weight, kept_modes, False)
    preact = local_part + spectral_part.astype(jnp.float32)
    weighted = (gelu_slope(preact, cotangent.astype(jnp.float32)) * fluid_mask).astype(jnp.bfloat16)
    spec_grad = spectral(weighted, spec_weight, kept_modes, True)
    ext_grad = with_halo(weighted, (("gx", 0),), 1)
    padded_grad = pad_sides(ext_grad)
    input_grad = jnp.einsum(
        "oc,xyoz->xycz", point_weight, weighted, preferred_element_type=jnp.float32
    )
    input_grad = input_grad + jnp.einsum(
        "oc,xyoz->xycz", lap_weight, laplace_ext(ext_grad), preferred_element_type=jnp.float32
    )
    input_grad = input_grad + spec_grad.astype(jnp.float32)
    tile_grads = []
    for tile in range(tile_total):
        back_moved = window_of(padded_grad, offsets[tile], -1, weighted.shape)
        input_grad = input_grad + jnp.einsum(
            "oc,xyoz->xycz", kernel_weight[tile], back_moved, preferred_element_type=jnp.float32
        )
        tile_grads.append(
            jnp.einsum("xyoz,xycz->oc", back_moved, features, preferred_element_type=jnp.float32)
        )
    local_grad = jnp.stack(tile_grads, axis=0)
    scaling = float(
        lax.axis_size("gx") * features.shape[0] * features.shape[1] * features.shape[3]
    ) ** (-0.5)
    summed = sum_over_gx(local_grad)
    return (input_grad.astype(jnp.bfloat16), summed * scaling)


def solution(mesh):
    return jax.shard_map(
        per_device,
        mesh=mesh,
        in_specs=(
            P(("groups", "gx"), None, None, None),
            P(("groups", "gx"), None, None, None),
            P(("groups", "gx"), None, None),
            P(),
            P(),
            P(),
            P(),
            P(),
            P(),
            P(),
        ),
        out_specs=(P(("groups", "gx"), None, None, None), P("groups", None, None)),
        check_vma=False,
    )
```

profile of v0, /device:TPU:0, one launch (start us, length us, event | category | flops | bytes accessed | tf_op | source)
XLA Modules:
  0.0 166.4 jit_solution(13771764491910680602)
XLA Ops:
  0.7 1.1 fusion.148
  1.8 2.4 %collective-permute-start = (bf16[1,16,64,128]{3,2,1,0:T(8,128)(2,1)S(1)}, bf16[1,16,64,128]{3,2,1,0:T(8,128)(2,1)S(1)}, u32[]{:S(2)}, u32[]{:S(2)}) collective-permute-start(bf16[1,16,64,128]{3,2,1,0:T(8,128)(2,1)S(1)} %get-tuple-element.5), channel_id=1, source_target_pairs={{0,1},{1,2},{2,3},{3,4},{4,5},{5,6},{6,7},{7,8},{8,9},{9,10},{10,1... | collective-permute-start | bytes 786440 | tf_op jit(solution)/shard_map/ppermute | solution.py:19
  4.2 1.3 collective-permute-start.1
  5.5 1.9 %copy.40 = bf16[2,16,64,128]{3,2,0,1:T(8,128)(2,1)} copy(bf16[2,16,64,128]{3,2,1,0:T(8,128)(2,1)} %param.10) | data formatting | bytes 1048576 | tf_op args[0]
  7.4 9.4 %all-to-all-start = ((bf16[2,16,64,128]{3,2,0,1:T(8,128)(2,1)}), bf16[2,16,64,128]{3,2,0,1:T(8,128)(2,1)S(1)}, u32[]{:S(2)}, u32[]{:S(2)}) async-start(bf16[2,16,64,128]{3,2,0,1:T(8,128)(2,1)} %copy.40), calls=%async_computation | async-start | bytes 1048576 | tf_op jit(solution)/shard_map/all_to_all | solution.py:58
  16.9 1.3 fusion.76
  18.1 0.5 compare_select_fusion
  18.7 0.7 fusion.149
  19.4 0.6 multiply_add_fusion
  42.5 0.5 fusion.47
  42.9 1.5 fusion.48
  44.4 1.4 fusion.49
  45.8 1.1 convolution_convert_fusion.4
  47.2 1.1 fusion.17
  48.3 1.0 copy.44
  49.3 6.0 %all-to-all-start.1 = ((bf16[32,1,64,128]{3,2,1,0:T(8,128)(2,1)}), bf16[32,1,64,128]{3,2,1,0:T(8,128)(2,1)S(1)}, u32[]{:S(2)}, u32[]{:S(2)}) async-start(bf16[32,1,64,128]{3,2,1,0:T(8,128)(2,1)} %copy.44), calls=%async_computation.1 | async-start | bytes 1048576 | tf_op jit(solution)/shard_map/all_to_all | solution.py:63
  55.3 0.8 pad_convert_fusion.1
  56.1 1.4 fusion.50
  57.5 1.4 fusion.51
  58.9 2.8 %convolution_add_fusion.1 = f32[2,16,128,64]{2,3,1,0:T(8,128)} fusion(f32[2,16,128,64]{2,3,1,0:T(8,128)S(1)} %copy-done.4, f32[4,18,64,130]{3,2,1,0:T(8,128)S(1)} %pad_convert_fusion.1, bf16[64,64]{1,0:T(8,128)(2,1)S(1)} %copy-done.15), kind=kOutput, calls=%fused_computation.37 | convolution fusion | flops 35913728 | bytes 9453568 | tf_op jit(solution)/shard_map/oc,xycz->xyoz/dot_general | solution.py:128
  61.8 8.0 %all-to-all-done.1 = bf16[32,1,64,128]{3,2,1,0:T(8,128)(2,1)S(1)} async-done(((bf16[32,1,64,128]{3,2,1,0:T(8,128)(2,1)}), bf16[32,1,64,128]{3,2,1,0:T(8,128)(2,1)S(1)}, u32[]{:S(2)}, u32[]{:S(2)}) %all-to-all-start.1) | async-done | bytes 524320 | tf_op jit(solution)/shard_map/all_to_all | solution.py:63
  69.7 0.8 copy-done.3
  70.5 4.2 %fusion.33 = bf16[2,16,64,128]{3,2,1,0:T(8,128)(2,1)S(1)} fusion(bf16[2,16,64,128]{3,2,1,0:T(8,128)(2,1)} %param.11, f32[2,16,128,64]{2,3,1,0:T(8,128)} %fusion.51, f32[2,16,128,64]{2,3,1,0:T(8,128)} %fusion.50, f32[2,16,128,64]{2,3,1,0:T(8,128)} %fusion.49, f32[2,16,128,64]{2,3,1,0:T(8,128)} %fusion.48, f32[2,16,128,64]{2,3,1,0:T(8,128)S(1)} %fusion.47, ...), kind=kOutput, calls=%fused_computation.72 | convolution fusion | flops 41680896 | bytes 8946188 | tf_op jit(solution)/shard_map/oc,xycz->xyoz/dot_general | solution.py:133
  74.8 1.9 %collective-permute-start.2 = (bf16[1,16,64,128]{3,2,1,0:T(8,128)(2,1)S(1)}, bf16[1,16,64,128]{3,2,1,0:T(8,128)(2,1)S(1)}, u32[]{:S(2)}, u32[]{:S(2)}) collective-permute-start(bf16[1,16,64,128]{3,2,1,0:T(8,128)(2,1)S(1)} %get-tuple-element.2), channel_id=1, source_target_pairs={{0,1},{1,2},{2,3},{3,4},{4,5},{5,6},{6,7},{7,8},{8,9},{9,10},{10,1... | collective-permute-start | bytes 786440 | tf_op jit(solution)/shard_map/ppermute | solution.py:19
  76.7 1.3 collective-permute-start.3
  91.8 0.8 all_to_all.57
  92.6 6.9 %all-to-all-start.4 = ((f32[16,1,1536]{2,1,0:T(1,128)}), f32[16,1,1536]{2,1,0:T(1,128)S(1)}, u32[]{:S(2)}, u32[]{:S(2)}) async-start(f32[16,1,1536]{2,1,0:T(1,128)} %all_to_all.57), calls=%async_computation.4 | async-start | bytes 196608 | tf_op jit(solution)/shard_map/all_to_all | solution.py:98
  99.5 0.8 copy.49
  100.3 6.6 %all-to-all-done.4 = f32[16,1,1536]{2,1,0:T(1,128)S(1)} async-done(((f32[16,1,1536]{2,1,0:T(1,128)}), f32[16,1,1536]{2,1,0:T(1,128)S(1)}, u32[]{:S(2)}, u32[]{:S(2)}) %all-to-all-start.4) | async-done | bytes 98336 | tf_op jit(solution)/shard_map/all_to_all | solution.py:98
  106.9 0.6 copy-done.6
  107.6 3.8 %all-to-all-start.2 = ((bf16[2,16,64,128]{3,2,0,1:T(8,128)(2,1)}), bf16[2,16,64,128]{3,2,0,1:T(8,128)(2,1)S(1)}, u32[]{:S(2)}, u32[]{:S(2)}) async-start(bf16[2,16,64,128]{3,2,0,1:T(8,128)(2,1)} %copy.49), calls=%async_computation.2 | async-start | bytes 1048576 | tf_op jit(solution)/shard_map/all_to_all | solution.py:58
  111.4 1.3 fusion.74
  113.2 1.4 convolution_bitcast_fusion.2
  114.7 10.8 %all-to-all-done.2 = bf16[2,16,64,128]{3,2,0,1:T(8,128)(2,1)S(1)} async-done(((bf16[2,16,64,128]{3,2,0,1:T(8,128)(2,1)}), bf16[2,16,64,128]{3,2,0,1:T(8,128)(2,1)S(1)}, u32[]{:S(2)}, u32[]{:S(2)}) %all-to-all-start.2) | async-done | bytes 524320 | tf_op jit(solution)/shard_map/all_to_all | solution.py:58
  125.6 0.7 broadcast_in_dim.14
  126.3 4.0 %all-to-all-start.5 = ((f32[16,1,1536]{2,1,0:T(1,128)}), f32[16,1,1536]{2,1,0:T(1,128)S(1)}, u32[]{:S(2)}, u32[]{:S(2)}) async-start(f32[16,1,1536]{2,1,0:T(1,128)} %broadcast_in_dim.14), calls=%async_computation.5 | async-start | bytes 196608 | tf_op jit(solution)/shard_map/all_to_all | solution.py:101
  130.3 0.5 fusion.22
  131.5 1.0 copy.55
  132.5 5.2 %all-to-all-done.5 = f32[16,1,1536]{2,1,0:T(1,128)S(1)} async-done(((f32[16,1,1536]{2,1,0:T(1,128)}), f32[16,1,1536]{2,1,0:T(1,128)S(1)}, u32[]{:S(2)}, u32[]{:S(2)}) %all-to-all-start.5) | async-done | bytes 98336 | tf_op jit(solution)/shard_map/all_to_all | solution.py:101
  137.7 3.6 %all-to-all-start.3 = ((bf16[32,1,64,128]{3,2,1,0:T(8,128)(2,1)}), bf16[32,1,64,128]{3,2,1,0:T(8,128)(2,1)S(1)}, u32[]{:S(2)}, u32[]{:S(2)}) async-start(bf16[32,1,64,128]{3,2,1,0:T(8,128)(2,1)} %copy.55), calls=%async_computation.3 | async-start | bytes 1048576 | tf_op jit(solution)/shard_map/all_to_all | solution.py:63
  141.3 2.9 %pad_convert_fusion = f32[4,18,64,130]{3,2,1,0:T(8,128)} fusion(bf16[4,16,64,128]{3,2,1,0:T(8,128)(2,1)S(1)} %pad_maximum_fusion), kind=kLoop, calls=%fused_computation.12 | loop fusion | flops 599040 | bytes 3444736 | tf_op jit(solution)/shard_map/convert_element_type | solution.py:67
  144.2 1.4 convolution_bitcast_fusion.3
  145.6 1.5 convolution_bitcast_fusion.4
  147.1 1.4 convolution_bitcast_fusion
  148.7 0.8 mul.295
  149.5 6.2 %all-to-all-done.3 = bf16[32,1,64,128]{3,2,1,0:T(8,128)(2,1)S(1)} async-done(((bf16[32,1,64,128]{3,2,1,0:T(8,128)(2,1)}), bf16[32,1,64,128]{3,2,1,0:T(8,128)(2,1)S(1)}, u32[]{:S(2)}, u32[]{:S(2)}) %all-to-all-start.3) | async-done | bytes 524320 | tf_op jit(solution)/shard_map/all_to_all | solution.py:63
  155.7 7.5 %fusion.15 = f32[2,16,64,128]{3,2,1,0:T(8,128)S(1)} fusion(f32[2,16,128,64]{2,3,1,0:T(8,128)} %fusion.74, f32[4,18,64,130]{3,2,1,0:T(8,128)} %pad_convert_fusion, bf16[64,64]{1,0:T(8,128)(2,1)S(1)} %copy-done.16, bf16[16,2,1,64,128]{4,3,1,0,2:T(8,128)(2,1)S(1)} %bitcast.307), kind=kOutput, calls=%fused_computation.40 | convolution fusion | flops 36438016 | bytes 9969664 | tf_op jit(solution)/shard_map/oc,xyoz->xycz/dot_general | solution.py:146
  163.2 3.2 %fusion.16 = bf16[2,16,64,128]{3,2,1,0:T(8,128)(2,1)} fusion(f32[2,16,64,128]{3,2,1,0:T(8,128)S(1)} %copy-done.2, f32[2,16,64,128]{3,2,1,0:T(8,128)S(1)} %convolution_bitcast_fusion.1, f32[2,16,64,128]{3,2,1,0:T(8,128)} %convolution_bitcast_fusion.2, f32[2,16,64,128]{3,2,1,0:T(8,128)} %convolution_bitcast_fusion.3, ...), kind=kOutput, calls=%fused_computation.43 | convolution fusion | flops 35389440 | bytes 7880716 | tf_op jit(solution)/shard_map/oc,xyoz->xycz/dot_general | solution.py:153
  (57 shorter events, 4.6 us)
Async XLA Ops:
  0.6 46.3 %copy-start = (bf16[16,64,64]{2,1,0:T(8,128)(2,1)S(1)}, bf16[16,64,64]{2,1,0:T(8,128)(2,1)}, u32[]{:S(2)}) copy-start(bf16[16,64,64]{2,1,0:T(8,128)(2,1)} %param.18) | copy-start | bytes 393220
  0.6 16.2 %copy-start.1 = (bf16[2,16,64,128]{3,2,1,0:T(8,128)(2,1)S(1)}, bf16[2,16,64,128]{3,2,1,0:T(8,128)(2,1)}, u32[]{:S(2)}) copy-start(bf16[2,16,64,128]{3,2,1,0:T(8,128)(2,1)} %param.10) | copy-start | bytes 1572868
  0.7 16.2 %copy-start.14 = (s32[64]{0:T(128)S(1)}, s32[64]{0:T(128)}, u32[]{:S(2)}) copy-start(s32[64]{0:T(128)} %param.13) | copy-start | bytes 772
  0.7 16.2 %copy-start.8 = (bf16[64,64]{1,0:T(8,128)(2,1)S(1)}, bf16[64,64]{1,0:T(8,128)(2,1)}, u32[]{:S(2)}) copy-start(bf16[64,64]{1,0:T(8,128)(2,1)} %param.15) | copy-start | bytes 24580
  0.7 17.4 %copy-start.10 = (s32[2,16,128]{2,1,0:T(8,128)S(1)}, s32[2,16,128]{2,1,0:T(8,128)}, u32[]{:S(2)}) copy-start(s32[2,16,128]{2,1,0:T(8,128)} %param.12) | copy-start | bytes 49156
  0.7 18.0 %copy-start.9 = (s32[6,3]{0,1:T(4,128)S(1)}, s32[6,3]{0,1:T(4,128)}, u32[]{:S(2)}) copy-start(s32[6,3]{0,1:T(4,128)} %param.14) | copy-start | bytes 220
  1.8 40.5 %collective-permute-start = (bf16[1,16,64,128]{3,2,1,0:T(8,128)(2,1)S(1)}, bf16[1,16,64,128]{3,2,1,0:T(8,128)(2,1)S(1)}, u32[]{:S(2)}, u32[]{:S(2)}) collective-permute-start(bf16[1,16,64,128]{3,2,1,0:T(8,128)(2,1)S(1)} %get-tuple-element.5), channel_id=1, source_target_pairs={{0,1},{1,2},{2,3},{3,4},{4,5},{5,6},{6,7},{7,8},{8,9},{9,10},{10,1... | collective-permute-start | bytes 786440 | tf_op jit(solution)/shard_map/ppermute | solution.py:19
  4.2 38.2 %collective-permute-start.1 = (bf16[1,16,64,128]{3,2,1,0:T(8,128)(2,1)S(1)}, bf16[1,16,64,128]{3,2,1,0:T(8,128)(2,1)S(1)}, u32[]{:S(2)}, u32[]{:S(2)}) collective-permute-start(bf16[1,16,64,128]{3,2,1,0:T(8,128)(2,1)S(1)} %get-tuple-element.4), channel_id=1, source_target_pairs={{1,0},{2,1},{3,2},{4,3},{5,4},{6,5},{7,6},{8,7},{9,8},{10,9},{11,1... | collective-permute-start | bytes 786440 | tf_op jit(solution)/shard_map/ppermute | solution.py:21
  7.4 35.1 %copy-start.5 = (bf16[6,64,64]{2,1,0:T(8,128)(2,1)S(1)}, bf16[6,64,64]{2,1,0:T(8,128)(2,1)}, u32[]{:S(2)}) copy-start(bf16[6,64,64]{2,1,0:T(8,128)(2,1)} %param.16) | copy-start | bytes 147460
  7.4 38.4 %all-to-all-start = ((bf16[2,16,64,128]{3,2,0,1:T(8,128)(2,1)}), bf16[2,16,64,128]{3,2,0,1:T(8,128)(2,1)S(1)}, u32[]{:S(2)}, u32[]{:S(2)}) async-start(bf16[2,16,64,128]{3,2,0,1:T(8,128)(2,1)} %copy.40), calls=%async_computation | async-start | bytes 1048576 | tf_op jit(solution)/shard_map/all_to_all | solution.py:58
  49.3 20.5 %all-to-all-start.1 = ((bf16[32,1,64,128]{3,2,1,0:T(8,128)(2,1)}), bf16[32,1,64,128]{3,2,1,0:T(8,128)(2,1)S(1)}, u32[]{:S(2)}, u32[]{:S(2)}) async-start(bf16[32,1,64,128]{3,2,1,0:T(8,128)(2,1)} %copy.44), calls=%async_computation.1 | async-start | bytes 1048576 | tf_op jit(solution)/shard_map/all_to_all | solution.py:63
  56.0 2.9 %copy-start.4 = (f32[2,16,128,64]{2,3,1,0:T(8,128)S(1)}, f32[2,16,128,64]{2,3,1,0:T(8,128)}, u32[]{:S(2)}) copy-start(f32[2,16,128,64]{2,3,1,0:T(8,128)} %fusion.76) | copy-start | bytes 3145732
  56.1 2.9 %copy-start.15 = (bf16[64,64]{1,0:T(8,128)(2,1)S(1)}, bf16[64,64]{1,0:T(8,128)(2,1)}, u32[]{:S(2)}) copy-start(bf16[64,64]{1,0:T(8,128)(2,1)} %param.17) | copy-start | bytes 24580
  57.5 13.0 %copy-start.13 = (f32[64]{0:T(128)S(1)}, f32[64]{0:T(128)}, u32[]{:S(2)}) copy-start(f32[64]{0:T(128)} %param.19) | copy-start | bytes 772
  69.7 0.8 copy-start.3
  74.8 14.5 %collective-permute-start.2 = (bf16[1,16,64,128]{3,2,1,0:T(8,128)(2,1)S(1)}, bf16[1,16,64,128]{3,2,1,0:T(8,128)(2,1)S(1)}, u32[]{:S(2)}, u32[]{:S(2)}) collective-permute-start(bf16[1,16,64,128]{3,2,1,0:T(8,128)(2,1)S(1)} %get-tuple-element.2), channel_id=1, source_target_pairs={{0,1},{1,2},{2,3},{3,4},{4,5},{5,6},{6,7},{7,8},{8,9},{9,10},{10,1... | collective-permute-start | bytes 786440 | tf_op jit(solution)/shard_map/ppermute | solution.py:19
  76.7 12.6 %collective-permute-start.3 = (bf16[1,16,64,128]{3,2,1,0:T(8,128)(2,1)S(1)}, bf16[1,16,64,128]{3,2,1,0:T(8,128)(2,1)S(1)}, u32[]{:S(2)}, u32[]{:S(2)}) collective-permute-start(bf16[1,16,64,128]{3,2,1,0:T(8,128)(2,1)S(1)} %get-tuple-element.3), channel_id=1, source_target_pairs={{1,0},{2,1},{3,2},{4,3},{5,4},{6,5},{7,6},{8,7},{9,8},{10,9},{11,1... | collective-permute-start | bytes 786440 | tf_op jit(solution)/shard_map/ppermute | solution.py:21
  92.6 14.3 %all-to-all-start.4 = ((f32[16,1,1536]{2,1,0:T(1,128)}), f32[16,1,1536]{2,1,0:T(1,128)S(1)}, u32[]{:S(2)}, u32[]{:S(2)}) async-start(f32[16,1,1536]{2,1,0:T(1,128)} %all_to_all.57), calls=%async_computation.4 | async-start | bytes 196608 | tf_op jit(solution)/shard_map/all_to_all | solution.py:98
  106.9 0.6 copy-start.6
  107.6 18.0 %all-to-all-start.2 = ((bf16[2,16,64,128]{3,2,0,1:T(8,128)(2,1)}), bf16[2,16,64,128]{3,2,0,1:T(8,128)(2,1)S(1)}, u32[]{:S(2)}, u32[]{:S(2)}) async-start(bf16[2,16,64,128]{3,2,0,1:T(8,128)(2,1)} %copy.49), calls=%async_computation.2 | async-start | bytes 1048576 | tf_op jit(solution)/shard_map/all_to_all | solution.py:58
  112.8 1.9 %copy-start.7 = (f32[16,1,1536]{2,1,0:T(1,128)S(1)}, f32[16,1,1536]{2,1,0:T(1,128)}, u32[]{:S(2)}) copy-start(f32[16,1,1536]{2,1,0:T(1,128)} %copy-done.6) | copy-start | bytes 294916
  112.8 17.5 %copy-start.11 = (f32[16]{0:T(128)S(1)}, f32[16]{0:T(128)}, u32[]{:S(2)}) copy-start(f32[16]{0:T(128)} %get-tuple-element.27) | copy-start | bytes 196
  112.8 17.5 %copy-start.12 = (f32[32]{0:T(128)S(1)}, f32[32]{0:T(128)}, u32[]{:S(2)}) copy-start(f32[32]{0:T(128)} %multiply_add_fusion) | copy-start | bytes 388
  126.3 11.4 %all-to-all-start.5 = ((f32[16,1,1536]{2,1,0:T(1,128)}), f32[16,1,1536]{2,1,0:T(1,128)S(1)}, u32[]{:S(2)}, u32[]{:S(2)}) async-start(f32[16,1,1536]{2,1,0:T(1,128)} %broadcast_in_dim.14), calls=%async_computation.5 | async-start | bytes 196608 | tf_op jit(solution)/shard_map/all_to_all | solution.py:101
  137.7 18.0 %all-to-all-start.3 = ((bf16[32,1,64,128]{3,2,1,0:T(8,128)(2,1)}), bf16[32,1,64,128]{3,2,1,0:T(8,128)(2,1)S(1)}, u32[]{:S(2)}, u32[]{:S(2)}) async-start(bf16[32,1,64,128]{3,2,1,0:T(8,128)(2,1)} %copy.55), calls=%async_computation.3 | async-start | bytes 1048576 | tf_op jit(solution)/shard_map/all_to_all | solution.py:63
  145.6 10.1 %copy-start.16 = (bf16[64,64]{1,0:T(8,128)(2,1)S(1)}, bf16[64,64]{1,0:T(8,128)(2,1)}, u32[]{:S(2)}) copy-start(bf16[64,64]{1,0:T(8,128)(2,1)} %param.17) | copy-start | bytes 24580
  155.7 7.5 %copy-start.2 = (f32[2,16,64,128]{3,2,1,0:T(8,128)S(1)}, f32[2,16,64,128]{3,2,1,0:T(8,128)}, u32[]{:S(2)}) copy-start(f32[2,16,64,128]{3,2,1,0:T(8,128)} %convolution_bitcast_fusion) | copy-start | bytes 3145732
where the time goes:
time: 168 us; the launch traced here: 166 us
  starting transfers between devices  40.5 us (24%)
  matrix products  38.7 us (23%)
  waiting for transfers between devices  36.7 us (22%)
  between operations  34.7 us (21%)
  local copies, waits for them, and re-layouts  10.6 us (6%)
  other arithmetic  5.23 us (3%)
    all_to_all x2, waiting for transfers between devices, spectral(): return lax.all_to_all(result, 'gx', split_axis=0, concat_axis=1, tiled=True)  14.1 us
    all_to_all x2, starting transfers between devices, spectral(): lax.all_to_all(slab, 'gx', split_axis=1, concat_axis=0, tiled=True)  13.2 us
    all_to_all x2, waiting for transfers between devices, spectral(): lax.all_to_all(slab, 'gx', split_axis=1, concat_axis=0, tiled=True)  10.8 us
    dot_general x6, matrix products, per_device(): jnp.einsum('oc,xycz->xyoz', kernel_weight[tile], moved, preferred_element...  10.4 us
    all_to_all x2, starting transfers between devices, spectral(): return lax.all_to_all(result, 'gx', split_axis=0, concat_axis=1, tiled=True)  9.56 us
    dot_general x6, matrix products, per_device(): jnp.einsum('oc,xyoz->xycz', kernel_weight[tile], back_moved, preferred_el...  9.38 us
    dot_general x1, matrix products, per_device(): jnp.einsum('oc,xyoz->xycz', lap_weight, laplace_ext(ext_grad), preferred_...  7.47 us
    all_to_all x1, starting transfers between devices, sum_over_gx(): lax.all_to_all(terms.reshape(count, -1), 'gx', split_axis=0, concat_axis=...  6.87 us
  transfers between devices with their start and end apart: 10, of which 5 were waited for; matrix products, arithmetic and copies ran while one was open for 18% of the time, Pallas kernels for 0%

commit v1 on v0

--- a/solution.py
+++ b/solution.py
@@ -4,6 +4,7 @@
 import jax.numpy as jnp
 from jax import lax
 from jax.sharding import PartitionSpec as P
+from jax.lax import all_to_all, axis_size
 
 RAD = 2
 
@@ -55,7 +56,15 @@
 
 def spectral(slab, spec_weight, kept_modes, adjoint):
     result = pencil_work(
-        lax.all_to_all(slab, "gx", split_axis=1, concat_axis=0, tiled=True),
+        jnp.concatenate(
+            all_to_all(
+                jnp.stack(jnp.split(slab, axis_size("gx"), 1), 0),
+                axis_name="gx",
+                split_axis=0,
+                concat_axis=0,
+            ),
+            axis=0,
+        ),
         spec_weight,
         kept_modes,
         adjoint,

time: 168 us -> 198 us (1.18)
  local copies, waits for them, and re-layouts: 10.6 us -> 39.6 us
    unnamed x37 -> x62, local copies, waits for them, and re-layouts: 3.47 us -> 30.8 us
    another operation x0 -> x2, local copies, waits for them, and re-layouts: none -> 2 us  [spectral(): jnp.stack(jnp.split(slab, axis_size('gx'), 1), 0)]
  transfers between devices with their start and end apart: 10 -> 10, of which waited for: 5 -> 5; matrix products, arithmetic and copies ran while one was open for 18% -> 30% of each run, Pallas kernels for 0% -> 0%
where the time goes in v1:
time: 198 us; the launch traced here: 196 us
  starting transfers between devices  40.3 us (20%)
  local copies, waits for them, and re-layouts  39.6 us (20%)
  matrix products  38.6 us (19%)
  waiting for transfers between devices  37.1 us (19%)
  between operations  35.1 us (18%)
  other arithmetic  5.24 us (3%)
    unnamed x62, local copies, waits for them, and re-layouts  30.8 us
    all_to_all x2, waiting for transfers between devices, spectral(): return lax.all_to_all(result, 'gx', split_axis=0, concat_axis=1, tiled=True)  14.1 us
    all_to_all x2, starting transfers between devices, spectral(): all_to_all(jnp.stack(jnp.split(slab, axis_size('gx'), 1), 0), axis_name='...  13 us
    all_to_all x2, waiting for transfers between devices, spectral(): all_to_all(jnp.stack(jnp.split(slab, axis_size('gx'), 1), 0), axis_name='...  11.1 us
    dot_general x6, matrix products, per_device(): jnp.einsum('oc,xycz->xyoz', kernel_weight[tile], moved, preferred_element...  10.3 us
    all_to_all x2, starting transfers between devices, spectral(): return lax.all_to_all(result, 'gx', split_axis=0, concat_axis=1, tiled=True)  9.58 us
    dot_general x6, matrix products, per_device(): jnp.einsum('oc,xyoz->xycz', kernel_weight[tile], back_moved, preferred_el...  9.37 us
    dot_general x1, matrix products, per_device(): jnp.einsum('oc,xyoz->xycz', lap_weight, laplace_ext(ext_grad), preferred_...  7.5 us
  transfers between devices with their start and end apart: 10, of which 5 were waited for; matrix products, arithmetic and copies ran while one was open for 30% of the time, Pallas kernels for 0%

profile of v1, /device:TPU:0, one launch (start us, length us, event | category | flops | bytes accessed | tf_op | source)
XLA Modules:
  0.0 196.0 jit_solution(9809728871089283721)
XLA Ops:
  0.7 1.1 fusion.147
  1.8 2.4 %collective-permute-start = (bf16[1,16,64,128]{3,2,1,0:T(8,128)(2,1)S(1)}, bf16[1,16,64,128]{3,2,1,0:T(8,128)(2,1)S(1)}, u32[]{:S(2)}, u32[]{:S(2)}) collective-permute-start(bf16[1,16,64,128]{3,2,1,0:T(8,128)(2,1)S(1)} %get-tuple-element.5), channel_id=1, source_target_pairs={{0,1},{1,2},{2,3},{3,4},{4,5},{5,6},{6,7},{7,8},{8,9},{9,10},{10,1... | collective-permute-start | bytes 786440 | tf_op jit(solution)/shard_map/ppermute | solution.py:20
  4.2 1.3 collective-permute-start.1
  5.5 1.4 constant_dynamic-update-slice_fusion.18
  6.9 1.4 constant_dynamic-update-slice_fusion.17
  8.3 1.4 constant_dynamic-update-slice_fusion.16
  9.6 1.4 constant_dynamic-update-slice_fusion.15
  11.0 1.4 constant_dynamic-update-slice_fusion.14
  12.4 1.4 constant_dynamic-update-slice_fusion.13
  13.8 1.4 constant_dynamic-update-slice_fusion.12
  15.1 1.4 constant_dynamic-update-slice_fusion.11
  16.5 1.4 constant_dynamic-update-slice_fusion.10
  17.9 1.4 constant_dynamic-update-slice_fusion.9
  19.3 1.4 constant_dynamic-update-slice_fusion.8
  20.6 1.4 constant_dynamic-update-slice_fusion.7
  22.0 1.4 constant_dynamic-update-slice_fusion.6
  23.4 1.4 constant_dynamic-update-slice_fusion.5
  24.8 1.4 constant_dynamic-update-slice_fusion.4
  26.1 1.4 constant_dynamic-update-slice_fusion.3
  27.5 9.4 %all-to-all-start = ((bf16[16,2,1,64,128]{4,3,1,2,0:T(8,128)(2,1)}), bf16[16,2,1,64,128]{4,3,1,2,0:T(8,128)(2,1)S(1)}, u32[]{:S(2)}, u32[]{:S(2)}) async-start(bf16[16,2,1,64,128]{4,3,1,2,0:T(8,128)(2,1)} %constant_dynamic-update-slice_fusion.3), calls=%async_computation | async-start | bytes 1048576 | tf_op jit(solution)/shard_map/all_to_all | solution.py:60
  37.0 1.3 fusion.75
  74.7 1.5 fusion.48
  76.1 1.4 fusion.49
  79.4 1.1 fusion.17
  81.5 6.0 %all-to-all-start.1 = ((bf16[32,1,64,128]{3,2,1,0:T(8,128)(2,1)}), bf16[32,1,64,128]{3,2,1,0:T(8,128)(2,1)S(1)}, u32[]{:S(2)}, u32[]{:S(2)}) async-start(bf16[32,1,64,128]{3,2,1,0:T(8,128)(2,1)} %copy.116), calls=%async_computation.1 | async-start | bytes 1048576 | tf_op jit(solution)/shard_map/all_to_all | solution.py:72
  88.3 1.4 fusion.50
  89.7 1.4 fusion.51
  91.2 2.9 %convolution_add_fusion.1 = f32[2,16,128,64]{2,3,1,0:T(8,128)} fusion(f32[2,16,128,64]{2,3,1,0:T(8,128)S(1)} %copy-done.4, f32[4,18,64,130]{3,2,1,0:T(8,128)S(1)} %pad_convert_fusion.1, bf16[64,64]{1,0:T(8,128)(2,1)S(1)} %copy-done.13), kind=kOutput, calls=%fused_computation.37 | convolution fusion | flops 35913728 | bytes 9453568 | tf_op jit(solution)/shard_map/oc,xycz->xyoz/dot_general | solution.py:137
  94.0 8.0 %all-to-all-done.1 = bf16[32,1,64,128]{3,2,1,0:T(8,128)(2,1)S(1)} async-done(((bf16[32,1,64,128]{3,2,1,0:T(8,128)(2,1)}), bf16[32,1,64,128]{3,2,1,0:T(8,128)(2,1)S(1)}, u32[]{:S(2)}, u32[]{:S(2)}) %all-to-all-start.1) | async-done | bytes 524320 | tf_op jit(solution)/shard_map/all_to_all | solution.py:72
  102.8 4.2 %fusion.33 = bf16[2,16,64,128]{3,2,1,0:T(8,128)(2,1)S(1)} fusion(bf16[2,16,64,128]{3,2,1,0:T(8,128)(2,1)} %param.11, f32[2,16,128,64]{2,3,1,0:T(8,128)} %fusion.51, f32[2,16,128,64]{2,3,1,0:T(8,128)} %fusion.50, f32[2,16,128,64]{2,3,1,0:T(8,128)} %fusion.49, f32[2,16,128,64]{2,3,1,0:T(8,128)} %fusion.48, f32[2,16,128,64]{2,3,1,0:T(8,128)S(1)} %fusion.47, ...), kind=kOutput, calls=%fused_computation.72 | convolution fusion | flops 41680896 | bytes 8946188 | tf_op jit(solution)/shard_map/oc,xycz->xyoz/dot_general | solution.py:142
  107.6 1.9 collective-permute-start.2
  109.6 1.3 collective-permute-start.3
  122.8 6.9 %all-to-all-start.4 = ((f32[16,1,1536]{2,1,0:T(1,128)}), f32[16,1,1536]{2,1,0:T(1,128)S(1)}, u32[]{:S(2)}, u32[]{:S(2)}) async-start(f32[16,1,1536]{2,1,0:T(1,128)} %all_to_all.37), calls=%async_computation.4 | async-start | bytes 196608 | tf_op jit(solution)/shard_map/all_to_all | solution.py:107
  130.3 6.8 %all-to-all-done.4 = f32[16,1,1536]{2,1,0:T(1,128)S(1)} async-done(((f32[16,1,1536]{2,1,0:T(1,128)}), f32[16,1,1536]{2,1,0:T(1,128)S(1)}, u32[]{:S(2)}, u32[]{:S(2)}) %all-to-all-start.4) | async-done | bytes 98336 | tf_op jit(solution)/shard_map/all_to_all | solution.py:107
  137.1 3.6 %all-to-all-start.2 = ((bf16[16,2,1,64,128]{4,3,1,2,0:T(8,128)(2,1)}), bf16[16,2,1,64,128]{4,3,1,2,0:T(8,128)(2,1)S(1)}, u32[]{:S(2)}, u32[]{:S(2)}) async-start(bf16[16,2,1,64,128]{4,3,1,2,0:T(8,128)(2,1)} %constant_dynamic-update-slice_fusion.19), calls=%async_computation.2 | async-start | bytes 1048576 | tf_op jit(solution)/shard_map/all_to_all | solution.py:60
  140.8 1.3 fusion.73
  142.6 1.4 convolution_bitcast_fusion.2
  144.1 11.0 %all-to-all-done.2 = bf16[16,2,1,64,128]{4,3,1,2,0:T(8,128)(2,1)S(1)} async-done(((bf16[16,2,1,64,128]{4,3,1,2,0:T(8,128)(2,1)}), bf16[16,2,1,64,128]{4,3,1,2,0:T(8,128)(2,1)S(1)}, u32[]{:S(2)}, u32[]{:S(2)}) %all-to-all-start.2) | async-done | bytes 524320 | tf_op jit(solution)/shard_map/all_to_all | solution.py:60
  155.8 4.0 %all-to-all-start.5 = ((f32[16,1,1536]{2,1,0:T(1,128)}), f32[16,1,1536]{2,1,0:T(1,128)S(1)}, u32[]{:S(2)}, u32[]{:S(2)}) async-start(f32[16,1,1536]{2,1,0:T(1,128)} %broadcast_in_dim.14), calls=%async_computation.5 | async-start | bytes 196608 | tf_op jit(solution)/shard_map/all_to_all | solution.py:110
  162.1 5.2 %all-to-all-done.5 = f32[16,1,1536]{2,1,0:T(1,128)S(1)} async-done(((f32[16,1,1536]{2,1,0:T(1,128)}), f32[16,1,1536]{2,1,0:T(1,128)S(1)}, u32[]{:S(2)}, u32[]{:S(2)}) %all-to-all-start.5) | async-done | bytes 98336 | tf_op jit(solution)/shard_map/all_to_all | solution.py:110
  167.3 3.6 %all-to-all-start.3 = ((bf16[32,1,64,128]{3,2,1,0:T(8,128)(2,1)}), bf16[32,1,64,128]{3,2,1,0:T(8,128)(2,1)S(1)}, u32[]{:S(2)}, u32[]{:S(2)}) async-start(bf16[32,1,64,128]{3,2,1,0:T(8,128)(2,1)} %copy.141), calls=%async_computation.3 | async-start | bytes 1048576 | tf_op jit(solution)/shard_map/all_to_all | solution.py:72
  170.8 2.9 %pad_convert_fusion = f32[4,18,64,130]{3,2,1,0:T(8,128)} fusion(bf16[4,16,64,128]{3,2,1,0:T(8,128)(2,1)S(1)} %pad_maximum_fusion), kind=kLoop, calls=%fused_computation.12 | loop fusion | flops 599040 | bytes 3444736 | tf_op jit(solution)/shard_map/convert_element_type | solution.py:76
  173.8 1.4 convolution_bitcast_fusion.3
  175.2 1.5 convolution_bitcast_fusion.4
  176.7 1.4 convolution_bitcast_fusion
  179.1 6.2 %all-to-all-done.3 = bf16[32,1,64,128]{3,2,1,0:T(8,128)(2,1)S(1)} async-done(((bf16[32,1,64,128]{3,2,1,0:T(8,128)(2,1)}), bf16[32,1,64,128]{3,2,1,0:T(8,128)(2,1)S(1)}, u32[]{:S(2)}, u32[]{:S(2)}) %all-to-all-start.3) | async-done | bytes 524320 | tf_op jit(solution)/shard_map/all_to_all | solution.py:72
  185.3 7.5 %fusion.15 = f32[2,16,64,128]{3,2,1,0:T(8,128)S(1)} fusion(f32[2,16,128,64]{2,3,1,0:T(8,128)} %fusion.73, f32[4,18,64,130]{3,2,1,0:T(8,128)} %pad_convert_fusion, bf16[64,64]{1,0:T(8,128)(2,1)S(1)} %copy-done.14, bf16[16,2,1,64,128]{4,3,1,0,2:T(8,128)(2,1)S(1)} %bitcast.456), kind=kOutput, calls=%fused_computation.40 | convolution fusion | flops 36438016 | bytes 9969664 | tf_op jit(solution)/shard_map/oc,xyoz->xycz/dot_general | solution.py:155
  192.8 3.2 %fusion.16 = bf16[2,16,64,128]{3,2,1,0:T(8,128)(2,1)} fusion(f32[2,16,64,128]{3,2,1,0:T(8,128)S(1)} %copy-done.2, f32[2,16,64,128]{3,2,1,0:T(8,128)S(1)} %convolution_bitcast_fusion.1, f32[2,16,64,128]{3,2,1,0:T(8,128)} %convolution_bitcast_fusion.2, f32[2,16,64,128]{3,2,1,0:T(8,128)} %convolution_bitcast_fusion.3, ...), kind=kOutput, calls=%fused_computation.43 | convolution fusion | flops 35389440 | bytes 7880716 | tf_op jit(solution)/shard_map/oc,xyoz->xycz/dot_general | solution.py:162
  (84 shorter events, 24.5 us)
Async XLA Ops:
  0.6 78.5 %copy-start = (bf16[16,64,64]{2,1,0:T(8,128)(2,1)S(1)}, bf16[16,64,64]{2,1,0:T(8,128)(2,1)}, u32[]{:S(2)}) copy-start(bf16[16,64,64]{2,1,0:T(8,128)(2,1)} %param.18) | copy-start | bytes 393220
  0.6 36.3 %copy-start.1 = (bf16[2,16,64,128]{3,2,1,0:T(8,128)(2,1)S(1)}, bf16[2,16,64,128]{3,2,1,0:T(8,128)(2,1)}, u32[]{:S(2)}) copy-start(bf16[2,16,64,128]{3,2,1,0:T(8,128)(2,1)} %param.10) | copy-start | bytes 1572868
  0.7 36.3 %copy-start.12 = (s32[64]{0:T(128)S(1)}, s32[64]{0:T(128)}, u32[]{:S(2)}) copy-start(s32[64]{0:T(128)} %param.13) | copy-start | bytes 772
  0.7 36.3 %copy-start.6 = (bf16[64,64]{1,0:T(8,128)(2,1)S(1)}, bf16[64,64]{1,0:T(8,128)(2,1)}, u32[]{:S(2)}) copy-start(bf16[64,64]{1,0:T(8,128)(2,1)} %param.15) | copy-start | bytes 24580
  0.7 37.6 %copy-start.8 = (s32[2,16,128]{2,1,0:T(8,128)S(1)}, s32[2,16,128]{2,1,0:T(8,128)}, u32[]{:S(2)}) copy-start(s32[2,16,128]{2,1,0:T(8,128)} %param.12) | copy-start | bytes 49156
  0.7 38.1 %copy-start.7 = (s32[6,3]{0,1:T(4,128)S(1)}, s32[6,3]{0,1:T(4,128)}, u32[]{:S(2)}) copy-start(s32[6,3]{0,1:T(4,128)} %param.14) | copy-start | bytes 220
  1.8 72.2 %collective-permute-start = (bf16[1,16,64,128]{3,2,1,0:T(8,128)(2,1)S(1)}, bf16[1,16,64,128]{3,2,1,0:T(8,128)(2,1)S(1)}, u32[]{:S(2)}, u32[]{:S(2)}) collective-permute-start(bf16[1,16,64,128]{3,2,1,0:T(8,128)(2,1)S(1)} %get-tuple-element.5), channel_id=1, source_target_pairs={{0,1},{1,2},{2,3},{3,4},{4,5},{5,6},{6,7},{7,8},{8,9},{9,10},{10,1... | collective-permute-start | bytes 786440 | tf_op jit(solution)/shard_map/ppermute | solution.py:20
  4.2 70.0 %collective-permute-start.1 = (bf16[1,16,64,128]{3,2,1,0:T(8,128)(2,1)S(1)}, bf16[1,16,64,128]{3,2,1,0:T(8,128)(2,1)S(1)}, u32[]{:S(2)}, u32[]{:S(2)}) collective-permute-start(bf16[1,16,64,128]{3,2,1,0:T(8,128)(2,1)S(1)} %get-tuple-element.4), channel_id=1, source_target_pairs={{1,0},{2,1},{3,2},{4,3},{5,4},{6,5},{7,6},{8,7},{9,8},{10,9},{11,1... | collective-permute-start | bytes 786440 | tf_op jit(solution)/shard_map/ppermute | solution.py:22
  27.5 46.7 %copy-start.5 = (bf16[6,64,64]{2,1,0:T(8,128)(2,1)S(1)}, bf16[6,64,64]{2,1,0:T(8,128)(2,1)}, u32[]{:S(2)}) copy-start(bf16[6,64,64]{2,1,0:T(8,128)(2,1)} %param.16) | copy-start | bytes 147460
  27.5 50.0 %all-to-all-start = ((bf16[16,2,1,64,128]{4,3,1,2,0:T(8,128)(2,1)}), bf16[16,2,1,64,128]{4,3,1,2,0:T(8,128)(2,1)S(1)}, u32[]{:S(2)}, u32[]{:S(2)}) async-start(bf16[16,2,1,64,128]{4,3,1,2,0:T(8,128)(2,1)} %constant_dynamic-update-slice_fusion.3), calls=%async_computation | async-start | bytes 1048576 | tf_op jit(solution)/shard_map/all_to_all | solution.py:60
  81.5 20.5 %all-to-all-start.1 = ((bf16[32,1,64,128]{3,2,1,0:T(8,128)(2,1)}), bf16[32,1,64,128]{3,2,1,0:T(8,128)(2,1)S(1)}, u32[]{:S(2)}, u32[]{:S(2)}) async-start(bf16[32,1,64,128]{3,2,1,0:T(8,128)(2,1)} %copy.116), calls=%async_computation.1 | async-start | bytes 1048576 | tf_op jit(solution)/shard_map/all_to_all | solution.py:72
  88.3 2.9 %copy-start.4 = (f32[2,16,128,64]{2,3,1,0:T(8,128)S(1)}, f32[2,16,128,64]{2,3,1,0:T(8,128)}, u32[]{:S(2)}) copy-start(f32[2,16,128,64]{2,3,1,0:T(8,128)} %fusion.75) | copy-start | bytes 3145732
  88.3 2.9 %copy-start.13 = (bf16[64,64]{1,0:T(8,128)(2,1)S(1)}, bf16[64,64]{1,0:T(8,128)(2,1)}, u32[]{:S(2)}) copy-start(bf16[64,64]{1,0:T(8,128)(2,1)} %param.17) | copy-start | bytes 24580
  89.7 13.0 %copy-start.11 = (f32[64]{0:T(128)S(1)}, f32[64]{0:T(128)}, u32[]{:S(2)}) copy-start(f32[64]{0:T(128)} %param.19) | copy-start | bytes 772
  102.0 0.8 copy-start.3
  107.6 11.9 %collective-permute-start.2 = (bf16[1,16,64,128]{3,2,1,0:T(8,128)(2,1)S(1)}, bf16[1,16,64,128]{3,2,1,0:T(8,128)(2,1)S(1)}, u32[]{:S(2)}, u32[]{:S(2)}) collective-permute-start(bf16[1,16,64,128]{3,2,1,0:T(8,128)(2,1)S(1)} %get-tuple-element.2), channel_id=1, source_target_pairs={{0,1},{1,2},{2,3},{3,4},{4,5},{5,6},{6,7},{7,8},{8,9},{9,10},{10,1... | collective-permute-start | bytes 786440 | tf_op jit(solution)/shard_map/ppermute | solution.py:20
  109.6 10.0 %collective-permute-start.3 = (bf16[1,16,64,128]{3,2,1,0:T(8,128)(2,1)S(1)}, bf16[1,16,64,128]{3,2,1,0:T(8,128)(2,1)S(1)}, u32[]{:S(2)}, u32[]{:S(2)}) collective-permute-start(bf16[1,16,64,128]{3,2,1,0:T(8,128)(2,1)S(1)} %get-tuple-element.3), channel_id=1, source_target_pairs={{1,0},{2,1},{3,2},{4,3},{5,4},{6,5},{7,6},{8,7},{9,8},{10,9},{11,1... | collective-permute-start | bytes 786440 | tf_op jit(solution)/shard_map/ppermute | solution.py:22
  122.8 14.3 %all-to-all-start.4 = ((f32[16,1,1536]{2,1,0:T(1,128)}), f32[16,1,1536]{2,1,0:T(1,128)S(1)}, u32[]{:S(2)}, u32[]{:S(2)}) async-start(f32[16,1,1536]{2,1,0:T(1,128)} %all_to_all.37), calls=%async_computation.4 | async-start | bytes 196608 | tf_op jit(solution)/shard_map/all_to_all | solution.py:107
  137.1 18.0 %all-to-all-start.2 = ((bf16[16,2,1,64,128]{4,3,1,2,0:T(8,128)(2,1)}), bf16[16,2,1,64,128]{4,3,1,2,0:T(8,128)(2,1)S(1)}, u32[]{:S(2)}, u32[]{:S(2)}) async-start(bf16[16,2,1,64,128]{4,3,1,2,0:T(8,128)(2,1)} %constant_dynamic-update-slice_fusion.19), calls=%async_computation.2 | async-start | bytes 1048576 | tf_op jit(solution)/shard_map/all_to_all | solution.py:60
  142.2 17.7 %copy-start.9 = (f32[16]{0:T(128)S(1)}, f32[16]{0:T(128)}, u32[]{:S(2)}) copy-start(f32[16]{0:T(128)} %get-tuple-element.27) | copy-start | bytes 196
  142.2 17.7 %copy-start.10 = (f32[32]{0:T(128)S(1)}, f32[32]{0:T(128)}, u32[]{:S(2)}) copy-start(f32[32]{0:T(128)} %multiply_add_fusion) | copy-start | bytes 388
  155.8 11.4 %all-to-all-start.5 = ((f32[16,1,1536]{2,1,0:T(1,128)}), f32[16,1,1536]{2,1,0:T(1,128)S(1)}, u32[]{:S(2)}, u32[]{:S(2)}) async-start(f32[16,1,1536]{2,1,0:T(1,128)} %broadcast_in_dim.14), calls=%async_computation.5 | async-start | bytes 196608 | tf_op jit(solution)/shard_map/all_to_all | solution.py:110
  167.3 18.0 %all-to-all-start.3 = ((bf16[32,1,64,128]{3,2,1,0:T(8,128)(2,1)}), bf16[32,1,64,128]{3,2,1,0:T(8,128)(2,1)S(1)}, u32[]{:S(2)}, u32[]{:S(2)}) async-start(bf16[32,1,64,128]{3,2,1,0:T(8,128)(2,1)} %copy.141), calls=%async_computation.3 | async-start | bytes 1048576 | tf_op jit(solution)/shard_map/all_to_all | solution.py:72
  175.2 10.1 %copy-start.14 = (bf16[64,64]{1,0:T(8,128)(2,1)S(1)}, bf16[64,64]{1,0:T(8,128)(2,1)}, u32[]{:S(2)}) copy-start(bf16[64,64]{1,0:T(8,128)(2,1)} %param.17) | copy-start | bytes 24580
  185.3 7.5 %copy-start.2 = (f32[2,16,64,128]{3,2,1,0:T(8,128)S(1)}, f32[2,16,64,128]{3,2,1,0:T(8,128)}, u32[]{:S(2)}) copy-start(f32[2,16,64,128]{3,2,1,0:T(8,128)} %convolution_bitcast_fusion) | copy-start | bytes 3145732
